TPU v7x, 32 devices: a whole 2x2x4 slice. The times are simulated.
32 devices in a mesh: gx: 8 (over z, y), gy: 4 (over x, core).
Axes of the slice: x: 2, y: 2, z: 4, core: 2. Of those that a mesh axis runs over, the one named last changes fastest.
Arguments:
- source_term: float32 [256, 128, 256], P('gx', 'gy'), may hold values from -6 to 6
- mobility_x: float32 [256, 128, 256], P('gx', 'gy'), may hold values from 0.001 to 1
- mobility_y: float32 [256, 128, 256], P('gx', 'gy'), may hold values from 0.001 to 1
- mobility_z: float32 [256, 128, 256], P('gx', 'gy'), may hold values from 0.001 to 1
- bubble_fraction: float32 [256, 128, 256], P('gx', 'gy'), may hold values from 0.1 to 1
- tile_labels: int32 [256, 128, 2], P('gx', 'gy'), may hold values from 0 to 65535, as said below
- send_tiles: int32 [32, 32, 128], P(('gx', 'gy')), may hold values from 0 to 2048, as said below
- recv_rows: int32 [32, 32, 128], P(('gx', 'gy')), may hold values from 0 to 2048, as said below
- block_inverse: float32 [512, 128, 128], P(('gx', 'gy'))
- couplings: float32 [512, 2, 128, 128], P(('gx', 'gy')), may hold values from -0.05303301 to 0.05303301
- neighbours: int32 [512, 2], P(('gx', 'gy')), may hold values from 0 to 511, as said below
Outputs:
- solution_field: float32 [256, 128, 256], P('gx', 'gy')
- residual: float32 [256, 128, 256], P('gx', 'gy')
Inputs may be any that keep to these rules, and one draw needn't show every extreme that they name: The tile_labels entry of a tile is o * 2048 + r exactly where its device s lists it in send_tiles[s, o, n] and recv_rows[o, s, n] = r; every tile is listed once. send_tiles[s, o, n] is a tile number of device s, or 2048 for an empty slot; the filled slots of each s and o come first; one owner receives 128 filled slots from every device. recv_rows[o, s, n] is the owned row that slot n from device s adds into, or 2048 where that slot is empty. Block q belongs to device q // 16. neighbours[q, n] is a block of another device. The entries listed by the blocks of one device name blocks of exactly 8 distinct devices, exactly 4 entries for each of them.
All inputs are finite; a program needn't handle non-finite values.
Results may differ from a plain program's by a relative error of at most 0.00012.
Values sent between devices are 32-bit elements; how exact they have to be, the bound alone decides.
A program may use at most 64 MiB of HBM per device.

v0:
```python
import jax
import jax.numpy as jnp
from jax import lax
from jax.sharding import PartitionSpec as P

TZ = 128
LINK = 4
ITERS = 2


def padded_2(block, sides, width):
    for axis, dim in sides:
        count = lax.axis_size(axis)
        forward = [(i, i + 1) for i in range(count - 1)]
        backward = [(target, source) for source, target in forward]
        low = lax.ppermute(
            lax.slice_in_dim(block, block.shape[dim] - width, None, axis=dim), axis, forward
        )
        high = lax.ppermute(lax.slice_in_dim(block, 0, width, axis=dim), axis, backward)
        block = jnp.concatenate([low, block, high], axis=dim)
    return block


def passed_along(value, axis, steps):
    count = lax.axis_size(axis)
    initial, last = (max(0, -steps), min(count, count - steps))
    return lax.ppermute(value, axis, [(source, source + steps) for source in range(initial, last)])


def lower_plane(values, axis):
    zero_plane = jnp.zeros_like(lax.slice_in_dim(values, 0, 1, axis=axis))
    return jnp.concatenate(
        [zero_plane, lax.slice_in_dim(values, 0, values.shape[axis] - 1, axis=axis)], axis=axis
    )


def upper_plane(values, axis):
    zero_plane = jnp.zeros_like(lax.slice_in_dim(values, 0, 1, axis=axis))
    return jnp.concatenate(
        [lax.slice_in_dim(values, 1, values.shape[axis], axis=axis), zero_plane], axis=axis
    )


def select_rows(positions, values):
    return jnp.take(values, positions, axis=0, mode="fill", fill_value=0.0)


def spread_rows(positions, values, out_count):
    empty = jnp.zeros((out_count,) + values.shape[1:], jnp.float32)
    return empty.at[positions].add(values, mode="drop")


def inner_total(left_field, right_field):
    return lax.psum(jnp.sum(left_field * right_field), ("gx", "gy"))


def apply_operator(field, mobility, lowers):
    padded = padded_2(field, (("gx", 0), ("gy", 1)), 1)
    part_x = mobility[0] * (padded[2:, 1:-1] - field) - lowers[0] * (field - padded[:-2, 1:-1])
    part_y = mobility[1] * (padded[1:-1, 2:] - field) - lowers[1] * (field - padded[1:-1, :-2])
    flux_z = mobility[2] * (upper_plane(field, 2) - field)
    part_z = flux_z - lower_plane(flux_z, 2)
    return -(part_x + part_y + part_z)


def precondition(resid, context):
    (
        bubble_fraction,
        tile_labels,
        send_list,
        recv_list,
        block_inverse,
        couplings,
        neighbours,
        diagonal,
    ) = context
    size_x, size_y, depth_z = resid.shape
    count_z = depth_z // TZ
    tile_totals = (
        (bubble_fraction * resid).reshape(size_x, size_y, count_z, TZ).sum(axis=3).reshape(-1)
    )
    tile_count = tile_totals.shape[0]
    blocks_here = block_inverse.shape[0]
    block_order = block_inverse.shape[1]
    rows_here = blocks_here * block_order
    width_x = lax.axis_size("gx")
    width_y = lax.axis_size("gy")
    device_count = width_x * width_y
    send_flat = send_list[0].reshape(-1)
    recv_flat = recv_list[0].reshape(-1)
    packed = select_rows(send_flat, tile_totals).reshape(send_list.shape[1], send_list.shape[2])
    arrived = lax.all_to_all(packed, ("gx", "gy"), split_axis=0, concat_axis=0, tiled=True)
    totals = spread_rows(recv_flat, arrived.reshape(-1), rows_here)
    totals = totals.reshape(blocks_here, block_order)
    sweep_one = jnp.einsum("qij,qj->qi", block_inverse, totals, precision=lax.Precision.HIGHEST)
    pushed = jnp.einsum("qkij,qj->qki", couplings, sweep_one, precision=lax.Precision.HIGHEST)
    flat_pushed = pushed.reshape(-1, block_order)
    flat_targets = neighbours.reshape(-1)
    target_device = flat_targets // blocks_here
    target_local = flat_targets % blocks_here
    push_count = flat_targets.shape[0]
    same = target_device[:, None] == target_device[None, :]
    earlier = jnp.arange(push_count)[None, :] < jnp.arange(push_count)[:, None]
    slot_rank = jnp.sum((same & earlier).astype(jnp.int32), axis=1)
    out_values = (
        jnp.zeros((device_count, LINK, block_order), jnp.float32)
        .at[target_device, slot_rank]
        .set(flat_pushed)
    )
    out_ids = (
        jnp.zeros((device_count, LINK), jnp.float32)
        .at[target_device, slot_rank]
        .set(target_local.astype(jnp.float32))
    )
    in_values, in_ids = (
        lax.all_to_all(out_values, ("gx", "gy"), split_axis=0, concat_axis=0, tiled=True),
        lax.all_to_all(out_ids, ("gx", "gy"), split_axis=0, concat_axis=0, tiled=True),
    )
    coupled = spread_rows(
        in_ids.reshape(-1).astype(jnp.int32), in_values.reshape(-1, block_order), blocks_here
    )
    sweep_two = jnp.einsum(
        "qij,qj->qi", block_inverse, totals - coupled, precision=lax.Precision.HIGHEST
    )
    outgoing = select_rows(recv_flat, sweep_two.reshape(-1)).reshape(
        recv_list.shape[1], recv_list.shape[2]
    )
    returned = lax.all_to_all(outgoing, ("gx", "gy"), split_axis=0, concat_axis=0, tiled=True)
    tile_values = spread_rows(send_flat, returned.reshape(-1), tile_count)
    spread = jnp.broadcast_to(
        tile_values.reshape(size_x, size_y, count_z, 1), (size_x, size_y, count_z, TZ)
    ).reshape(size_x, size_y, depth_z)
    return bubble_fraction * spread + resid / diagonal


def body(
    source_term,
    mobility_x,
    mobility_y,
    mobility_z,
    bubble_fraction,
    tile_labels,
    send_tiles,
    recv_rows,
    block_inverse,
    couplings,
    neighbours,
):
    lower_x = jnp.concatenate([passed_along(mobility_x[-1:], "gx", 1), mobility_x[:-1]], axis=0)
    lower_y = jnp.concatenate(
        [passed_along(mobility_y[:, -1:], "gy", 1), mobility_y[:, :-1]], axis=1
    )
    diagonal = (
        mobility_x + lower_x + (mobility_y + lower_y) + (mobility_z + lower_plane(mobility_z, 2))
    )
    mobility = (mobility_x, mobility_y, mobility_z)
    lowers = (lower_x, lower_y)
    context = (
        bubble_fraction,
        tile_labels,
        send_tiles,
        recv_rows,
        block_inverse,
        couplings,
        neighbours,
        diagonal,
    )
    solution_field = jnp.zeros_like(source_term)
    residual = source_term
    precond = precondition(residual, context)
    direction = precond
    rz_now = inner_total(residual, precond)
    for step in range(ITERS):
        image = apply_operator(direction, mobility, lowers)
        alpha = rz_now / inner_total(direction, image)
        solution_field = solution_field + alpha * direction
        residual = residual - alpha * image
        if step + 1 < ITERS:
            precond = precondition(residual, context)
            rz_next = inner_total(residual, precond)
            direction = precond + rz_next / rz_now * direction
            rz_now = rz_next
    return (solution_field, residual)


def solution(mesh):
    return jax.shard_map(
        body,
        mesh=mesh,
        in_specs=(
            P("gx", "gy", None),
            P("gx", "gy", None),
            P("gx", "gy", None),
            P("gx", "gy", None),
            P("gx", "gy", None),
            P("gx", "gy", None),
            P(("gx", "gy"), None, None),
            P(("gx", "gy"), None, None),
            P(("gx", "gy"), None, None),
            P(("gx", "gy"), None, None, None),
            P(("gx", "gy"), None),
        ),
        out_specs=(P("gx", "gy", None), P("gx", "gy", None)),
        check_vma=False,
    )
```

profile of v0, /device:TPU:0, one launch (start us, length us, event | category | flops | bytes accessed | tf_op | source)
XLA Modules:
  0.0 492.9 jit_solution(2808523701788882882)
XLA Ops:
  4.7 7.3 %all-to-all-start.1 = ((f32[32,1,4]{2,1,0:T(1,128)}), f32[32,1,4]{2,1,0:T(1,128)S(1)}, u32[]{:S(2)}, u32[]{:S(2)}) async-start(f32[32,1,4]{2,1,0:T(1,128)} %copy.23), calls=%async_computation.1 | async-start | bytes 32768 | tf_op jit(solution)/shard_map/all_to_all | solution.py:117
  25.8 23.0 %gather_fusion = f32[4096]{0:T(1024)S(1)} fusion(f32[2048]{0:T(1024)S(1)} %reshape.304, s32[4096]{0:T(1024)S(1)} %fusion.27), kind=kCustom, calls=%fused_computation.clone | custom fusion | bytes 49152 | tf_op jit(solution)/shard_map/jit(_take)/gather | solution.py:45
  49.5 5.1 %all-to-all-start = ((f32[32,1,128]{2,1,0:T(1,128)}), f32[32,1,128]{2,1,0:T(1,128)S(1)}, u32[]{:S(2)}, u32[]{:S(2)}) async-start(f32[32,1,128]{2,1,0:T(1,128)} %bitcast.6), calls=%async_computation | async-start | bytes 32768 | tf_op jit(solution)/shard_map/all_to_all | solution.py:92
  54.8 6.9 %all-to-all-done = f32[32,1,128]{2,1,0:T(1,128)S(1)} async-done(((f32[32,1,128]{2,1,0:T(1,128)}), f32[32,1,128]{2,1,0:T(1,128)S(1)}, u32[]{:S(2)}, u32[]{:S(2)}) %all-to-all-start) | async-done | bytes 16416 | tf_op jit(solution)/shard_map/all_to_all | solution.py:92
  61.7 21.9 %scatter_custom_fusion = f32[2048]{0:T(1024)S(1)} fusion(s32[4096]{0:T(1024)S(1)} %bitcast.122, f32[4096]{0:T(1024)S(1)} %bitcast.126, f32[]{:T(128)} %constant.33.clone.1), kind=kCustom, calls=%fused_computation.106 | custom fusion | flops 4096 | bytes 8196 | tf_op jit(solution)/shard_map/scatter-add | solution.py:50
  87.9 3.9 scatter_fusion.1
  94.4 7.4 %all-to-all-done.2 = f32[32,4,128]{2,1,0:T(4,128)S(1)} async-done(((f32[32,4,128]{2,1,0:T(4,128)}), f32[32,4,128]{2,1,0:T(4,128)S(1)}, u32[]{:S(2)}, u32[]{:S(2)}) %all-to-all-start.2) | async-done | bytes 65568 | tf_op jit(solution)/shard_map/all_to_all | solution.py:116
  104.8 23.0 %gather_fusion.1 = f32[4096]{0:T(1024)S(1)} fusion(f32[2048]{0:T(1024)S(1)} %bitcast.102, s32[4096]{0:T(1024)S(1)} %fusion.28), kind=kCustom, calls=%fused_computation.1.clone | custom fusion | bytes 49152 | tf_op jit(solution)/shard_map/jit(_take)/gather | solution.py:45
  132.3 5.8 %all-to-all-done.3 = f32[32,1,128]{2,1,0:T(1,128)S(1)} async-done(((f32[32,1,128]{2,1,0:T(1,128)}), f32[32,1,128]{2,1,0:T(1,128)S(1)}, u32[]{:S(2)}, u32[]{:S(2)}) %all-to-all-start.3) | async-done | bytes 16416 | tf_op jit(solution)/shard_map/all_to_all | solution.py:128
  138.1 22.0 %scatter_custom_fusion.4 = f32[2048]{0:T(1024)S(1)} fusion(s32[4096]{0:T(1024)S(1)} %bitcast.124, f32[4096]{0:T(1024)S(1)} %bitcast.127, f32[]{:T(128)} %constant.33.clone.1), kind=kCustom, calls=%fused_computation.104 | custom fusion | flops 4096 | bytes 8196 | tf_op jit(solution)/shard_map/scatter-add | solution.py:50
  165.4 5.8 %divide_add_fusion.1 = (f32[32,32,256]{2,1,0:T(8,128)S(1)}, f32[32,32,256]{2,1,0:T(8,128)}) fusion(f32[32,32,256]{2,1,0:T(8,128)} %param.13, f32[32,32,256]{2,1,0:T(8,128)} %param.17, f32[32,32,256]{2,1,0:T(8,128)} %reshape.313, f32[32,32,256]{2,1,0:T(8,128)} %param.16, f32[32,32,255]{2,1,0:T(8,128)} %bitcast.107, f32[32,32,256]{2,1,0:T(8,128)} %param.15, ...), kind=kLoop, calls=%fused_computation.70 | loop fusion | flops 2621440 | bytes 11530240 | tf_op jit(solution)/shard_map/add | solution.py:133
  172.6 4.5 collective-permute-start.3
  184.3 3.8 multiply_reduce_fusion.2
  188.1 41.7 %all-reduce.5 = (f32[]{:T(128)}, f32[]{:T(128)}) all-reduce(f32[]{:T(128)} %get-tuple-element.4, f32[]{:T(128)} %get-tuple-element.3), channel_id=1, replica_groups=mesh['gx'=8,'gy'=4] {'gx','gy'}, use_global_device_ids=true, to_apply=%region_8.10 | all-reduce | flops 2 | bytes 16 | tf_op jit(solution)/shard_map/psum | solution.py:54
  242.2 23.0 %gather_fusion.2 = f32[4096]{0:T(1024)S(1)} fusion(f32[2048]{0:T(1024)S(1)} %reshape.315, s32[4096]{0:T(1024)S(1)} %fusion.27), kind=kCustom, calls=%fused_computation.2.clone | custom fusion | bytes 49152 | tf_op jit(solution)/shard_map/jit(_take)/gather | solution.py:45
  265.2 12.3 %all_to_all.56 = f32[32,1,128]{2,1,0:T(1,128)S(1)} all-to-all(f32[32,1,128]{2,1,0:T(1,128)S(1)} %bitcast.118), channel_id=1, replica_groups=mesh['gx'=8,'gy'=4] {'gx','gy'}, dimensions={0} | all-to-all | bytes 32768 | tf_op jit(solution)/shard_map/all_to_all | solution.py:92
  277.5 22.1 %scatter_custom_fusion.5 = f32[2048]{0:T(1024)S(1)} fusion(s32[4096]{0:T(1024)S(1)} %bitcast.123, f32[4096]{0:T(1024)S(1)} %bitcast.129, f32[]{:T(128)} %constant.33.clone.1), kind=kCustom, calls=%fused_computation.102 | custom fusion | flops 4096 | bytes 8196 | tf_op jit(solution)/shard_map/scatter-add | solution.py:50
  306.6 9.1 %all_to_all.57 = f32[32,4,128]{2,1,0:T(4,128)S(1)} all-to-all(f32[32,4,128]{2,1,0:T(4,128)S(1)} %scatter_fusion.2), channel_id=1, replica_groups=mesh['gx'=8,'gy'=4] {'gx','gy'}, dimensions={0} | all-to-all | bytes 131072 | tf_op jit(solution)/shard_map/all_to_all | solution.py:116
  319.9 23.0 %gather_fusion.3 = f32[4096]{0:T(1024)S(1)} fusion(f32[2048]{0:T(1024)S(1)} %bitcast.101, s32[4096]{0:T(1024)S(1)} %fusion.28), kind=kCustom, calls=%fused_computation.3.clone | custom fusion | bytes 49152 | tf_op jit(solution)/shard_map/jit(_take)/gather | solution.py:45
  343.0 8.9 %all_to_all.58 = f32[32,1,128]{2,1,0:T(1,128)S(1)} all-to-all(f32[32,1,128]{2,1,0:T(1,128)S(1)} %bitcast.119), channel_id=1, replica_groups=mesh['gx'=8,'gy'=4] {'gx','gy'}, dimensions={0} | all-to-all | bytes 32768 | tf_op jit(solution)/shard_map/all_to_all | solution.py:128
  351.8 22.0 %scatter_custom_fusion.8 = f32[2048]{0:T(1024)S(1)} fusion(s32[4096]{0:T(1024)S(1)} %bitcast.125, f32[4096]{0:T(1024)S(1)} %bitcast.128, f32[]{:T(128)} %constant.33.clone.1), kind=kCustom, calls=%fused_computation.100 | custom fusion | flops 4096 | bytes 8196 | tf_op jit(solution)/shard_map/scatter-add | solution.py:50
  384.4 38.4 %psum.30 = f32[]{:T(128)} all-reduce(f32[]{:T(128)} %multiply_reduce_fusion.1), channel_id=1, replica_groups=mesh['gx'=8,'gy'=4] {'gx','gy'}, use_global_device_ids=true, to_apply=%region_17.19 | all-reduce | flops 1 | bytes 8 | tf_op jit(solution)/shard_map/psum | solution.py:54
  428.4 5.1 %collective-permute-start.7 = (f32[1,32,256]{2,1,0:T(8,128)S(1)}, f32[1,32,256]{2,1,0:T(8,128)S(1)}, u32[]{:S(2)}, u32[]{:S(2)}) collective-permute-start(f32[1,32,256]{2,1,0:T(8,128)S(1)} %get-tuple-element.22), channel_id=1, source_target_pairs={{0,4},{4,8},{8,12},{12,16},{16,20},{20,24},{24,28},{1,5},{5,9},{9,... | collective-permute-start | bytes 98312 | tf_op jit(solution)/shard_map/ppermute | solution.py:16
  444.3 43.4 %psum.31 = f32[]{:T(128)} all-reduce(f32[]{:T(128)} %get-tuple-element.7), channel_id=1, replica_groups=mesh['gx'=8,'gy'=4] {'gx','gy'}, use_global_device_ids=true, to_apply=%region_19.21 | all-reduce | flops 1 | bytes 8 | tf_op jit(solution)/shard_map/psum | solution.py:54
  (113 shorter events, 97.9 us)
Async XLA Ops:
  0.6 84.7 %copy-start = (f32[16,2,128,128]{3,2,1,0:T(8,128)S(1)}, f32[16,2,128,128]{3,2,1,0:T(8,128)}, u32[]{:S(2)}) copy-start(f32[16,2,128,128]{3,2,1,0:T(8,128)} %param.21) | copy-start | bytes 6291460
  4.7 44.8 %all-to-all-start.1 = ((f32[32,1,4]{2,1,0:T(1,128)}), f32[32,1,4]{2,1,0:T(1,128)S(1)}, u32[]{:S(2)}, u32[]{:S(2)}) async-start(f32[32,1,4]{2,1,0:T(1,128)} %copy.23), calls=%async_computation.1 | async-start | bytes 32768 | tf_op jit(solution)/shard_map/all_to_all | solution.py:117
  12.8 152.6 %collective-permute-start = (f32[1,32,256]{2,1,0:T(8,128)S(1)}, f32[1,32,256]{2,1,0:T(8,128)S(1)}, u32[]{:S(2)}, u32[]{:S(2)}) collective-permute-start(f32[1,32,256]{2,1,0:T(8,128)S(1)} %slice.83), channel_id=1, source_target_pairs={{0,4},{4,8},{8,12},{12,16},{16,20},{20,24},{24,28},{1,5},{5,9},{9,... | collective-permute-start | bytes 98312 | tf_op jit(solution)/shard_map/ppermute | solution.py:27
  17.4 148.0 %collective-permute-start.1 = (f32[32,1,256]{2,1,0:T(1,128)S(1)}, f32[32,1,256]{2,1,0:T(1,128)S(1)}, u32[]{:S(2)}, u32[]{:S(2)}) collective-permute-start(f32[32,1,256]{2,1,0:T(1,128)S(1)} %slice.85), channel_id=1, source_target_pairs={{0,1},{1,2},{2,3},{4,5},{5,6},{6,7},{8,9},{9,10},{10,11},{12,13},{... | collective-permute-start | bytes 98312 | tf_op jit(solution)/shard_map/ppermute | solution.py:27
  25.8 23.1 %copy-start.14 = (s32[1,32,128]{2,1,0:T(8,128)S(1)}, s32[1,32,128]{2,1,0:T(8,128)}, u32[]{:S(2)}) copy-start(s32[1,32,128]{2,1,0:T(8,128)} %param.18) | copy-start | bytes 49156
  25.8 23.7 %copy-start.13 = (s32[1,32,128]{2,1,0:T(8,128)S(1)}, s32[1,32,128]{2,1,0:T(8,128)}, u32[]{:S(2)}) copy-start(s32[1,32,128]{2,1,0:T(8,128)} %param.19) | copy-start | bytes 49156
  25.8 57.8 %copy-start.4 = (f32[16,128,128]{2,1,0:T(8,128)S(1)}, f32[16,128,128]{2,1,0:T(8,128)}, u32[]{:S(2)}) copy-start(f32[16,128,128]{2,1,0:T(8,128)} %param.20) | copy-start | bytes 3145732
  49.5 12.2 %all-to-all-start = ((f32[32,1,128]{2,1,0:T(1,128)}), f32[32,1,128]{2,1,0:T(1,128)S(1)}, u32[]{:S(2)}, u32[]{:S(2)}) async-start(f32[32,1,128]{2,1,0:T(1,128)} %bitcast.6), calls=%async_computation | async-start | bytes 32768 | tf_op jit(solution)/shard_map/all_to_all | solution.py:92
  91.8 10.0 %all-to-all-start.2 = ((f32[32,4,128]{2,1,0:T(4,128)}), f32[32,4,128]{2,1,0:T(4,128)S(1)}, u32[]{:S(2)}, u32[]{:S(2)}) async-start(f32[32,4,128]{2,1,0:T(4,128)} %scatter_fusion.1), calls=%async_computation.2 | async-start | bytes 131072 | tf_op jit(solution)/shard_map/all_to_all | solution.py:116
  104.8 26.4 %copy-start.6 = (f32[32,32,256]{2,1,0:T(8,128)S(1)}, f32[32,32,256]{2,1,0:T(8,128)}, u32[]{:S(2)}) copy-start(f32[32,32,256]{2,1,0:T(8,128)} %param.14) | copy-start | bytes 3145732
  128.5 9.7 %all-to-all-start.3 = ((f32[32,1,128]{2,1,0:T(1,128)}), f32[32,1,128]{2,1,0:T(1,128)S(1)}, u32[]{:S(2)}, u32[]{:S(2)}) async-start(f32[32,1,128]{2,1,0:T(1,128)} %bitcast.28), calls=%async_computation.3 | async-start | bytes 32768 | tf_op jit(solution)/shard_map/all_to_all | solution.py:128
  171.2 12.3 %copy-start.9 = (f32[32,32,256]{2,1,0:T(8,128)S(1)}, f32[32,32,256]{2,1,0:T(8,128)}, u32[]{:S(2)}) copy-start(f32[32,32,256]{2,1,0:T(8,128)} %param.16) | copy-start | bytes 3145732
  171.2 6.3 %collective-permute-start.2 = (f32[1,32,256]{2,1,0:T(8,128)S(1)}, f32[1,32,256]{2,1,0:T(8,128)S(1)}, u32[]{:S(2)}, u32[]{:S(2)}) collective-permute-start(f32[1,32,256]{2,1,0:T(8,128)S(1)} %get-tuple-element.25), channel_id=1, source_target_pairs={{4,0},{8,4},{12,8},{16,12},{20,16},{24,20},{28,24},{5,1},{9,5},{13... | collective-permute-start | bytes 98312 | tf_op jit(solution)/shard_map/ppermute | solution.py:19
  172.6 6.1 %collective-permute-start.3 = (f32[1,32,256]{2,1,0:T(8,128)S(1)}, f32[1,32,256]{2,1,0:T(8,128)S(1)}, u32[]{:S(2)}, u32[]{:S(2)}) collective-permute-start(f32[1,32,256]{2,1,0:T(8,128)S(1)} %get-tuple-element.24), channel_id=1, source_target_pairs={{0,4},{4,8},{8,12},{12,16},{16,20},{20,24},{24,28},{1,5},{5,9},{9,... | collective-permute-start | bytes 98312 | tf_op jit(solution)/shard_map/ppermute | solution.py:16
  178.8 4.9 %collective-permute-start.4 = (f32[34,1,256]{2,1,0:T(1,128)S(1)}, f32[34,1,256]{2,1,0:T(1,128)S(1)}, u32[]{:S(2)}, u32[]{:S(2)}) collective-permute-start(f32[34,1,256]{2,1,0:T(1,128)S(1)} %get-tuple-element.20), channel_id=1, source_target_pairs={{1,0},{2,1},{3,2},{5,4},{6,5},{7,6},{9,8},{10,9},{11,10},{13,12},{... | collective-permute-start | bytes 104456 | tf_op jit(solution)/shard_map/ppermute | solution.py:19
  180.1 4.2 copy-start.2
  180.1 4.2 copy-start.5
  180.2 4.1 collective-permute-start.5
  426.9 13.7 %copy-start.1 = (f32[32,32,256]{2,1,0:T(8,128)}, f32[32,32,256]{2,1,0:T(8,128)S(1)}, u32[]{:S(2)}) copy-start(f32[32,32,256]{2,1,0:T(8,128)S(1)} %multiply_add_fusion.1) | copy-start | bytes 3145732
  426.9 13.1 %copy-start.10 = (f32[32,32,256]{2,1,0:T(8,128)S(1)}, f32[32,32,256]{2,1,0:T(8,128)}, u32[]{:S(2)}) copy-start(f32[32,32,256]{2,1,0:T(8,128)} %param.16) | copy-start | bytes 3145732
  426.9 6.9 %collective-permute-start.6 = (f32[1,32,256]{2,1,0:T(8,128)S(1)}, f32[1,32,256]{2,1,0:T(8,128)S(1)}, u32[]{:S(2)}, u32[]{:S(2)}) collective-permute-start(f32[1,32,256]{2,1,0:T(8,128)S(1)} %get-tuple-element.23), channel_id=1, source_target_pairs={{4,0},{8,4},{12,8},{16,12},{20,16},{24,20},{28,24},{5,1},{9,5},{13... | collective-permute-start | bytes 98312 | tf_op jit(solution)/shard_map/ppermute | solution.py:19
  428.4 6.7 %collective-permute-start.7 = (f32[1,32,256]{2,1,0:T(8,128)S(1)}, f32[1,32,256]{2,1,0:T(8,128)S(1)}, u32[]{:S(2)}, u32[]{:S(2)}) collective-permute-start(f32[1,32,256]{2,1,0:T(8,128)S(1)} %get-tuple-element.22), channel_id=1, source_target_pairs={{0,4},{4,8},{8,12},{12,16},{16,20},{20,24},{24,28},{1,5},{5,9},{9,... | collective-permute-start | bytes 98312 | tf_op jit(solution)/shard_map/ppermute | solution.py:16
  435.1 5.2 %collective-permute-start.8 = (f32[34,1,256]{2,1,0:T(1,128)S(1)}, f32[34,1,256]{2,1,0:T(1,128)S(1)}, u32[]{:S(2)}, u32[]{:S(2)}) collective-permute-start(f32[34,1,256]{2,1,0:T(1,128)S(1)} %get-tuple-element.18), channel_id=1, source_target_pairs={{1,0},{2,1},{3,2},{5,4},{6,5},{7,6},{9,8},{10,9},{11,10},{13,12},{... | collective-permute-start | bytes 104456 | tf_op jit(solution)/shard_map/ppermute | solution.py:19
  436.4 4.1 collective-permute-start.9
  (5 other events, 20.9 us)
where the time goes:
time: 494 us; the launch traced here: 493 us
  blocking collectives  154 us (31%)
  other arithmetic  127 us (26%)
  local copies, waits for them, and re-layouts  125 us (25%)
  starting transfers between devices  45 us (9%)
  waiting for transfers between devices  23.4 us (5%)
  matrix products  13.1 us (3%)
  between operations  5.42 us (1%)
    psum x3, blocking collectives, inner_total(): return lax.psum(jnp.sum(left_field * right_field), ('gx', 'gy'))  124 us
    gather x4, local copies, waits for them, and re-layouts, select_rows(): return jnp.take(values, positions, axis=0, mode='fill', fill_value=0.0)  92.1 us
    scatter-add x6, other arithmetic, spread_rows(): return empty.at[positions].add(values, mode='drop')  90.5 us
    ppermute x4, starting transfers between devices, padded_2(): lax.ppermute(lax.slice_in_dim(block, block.shape[dim] - width, None, axis...  16.5 us
    all_to_all x1, blocking collectives, precondition(): lax.all_to_all(packed, ('gx', 'gy'), split_axis=0, concat_axis=0, tiled=T...  12.3 us
    reduce_sum x3, other arithmetic, inner_total(): return lax.psum(jnp.sum(left_field * right_field), ('gx', 'gy'))  10.7 us
  transfers between devices with their start and end apart: 14, of which 7 were waited for; matrix products, arithmetic and copies ran while one was open for 24% of the time, Pallas kernels for 0%

commit v1 on v0

v1 whole, which is shorter than its diff:
```python
import functools

import jax
import jax.numpy as jnp
from jax import lax
from jax.experimental import pallas as pl
from jax.experimental.pallas import tpu as pltpu
from jax.sharding import PartitionSpec as P

TZ = 128
LINK = 4
SLOT = 8
F32 = jnp.float32
BF16 = jnp.bfloat16
HIGHEST = lax.Precision.HIGHEST
MESH = pl.DeviceIdType.MESH
NT = (((1,), (1,)), ((), ()))
NN = (((1,), (0,)), ((), ()))
CELL_ARRAYS = 5


def log2(value):
    assert value & (value - 1) == 0
    return value.bit_length() - 1


def iota(shape, axis):
    return lax.broadcasted_iota(jnp.int32, shape, axis)


def split_three(value, axis=0):
    first = value.astype(BF16)
    rest = value - first.astype(F32)
    second = rest.astype(BF16)
    third = (rest - second.astype(F32)).astype(BF16)
    return jnp.concatenate([first, second, third], axis=axis)


def fold_three(value):
    third = value.shape[0] // 3
    return value[:third] + value[third : 2 * third] + value[2 * third :]


def one_hot_low(index):
    return jnp.where(iota((128, 128), 0) == (index & 127), 1.0, 0.0).astype(BF16)


def gather_rows(table, index_ref, out_ref, unroll):
    parts = split_three(table)
    high_count = table.shape[0]

    def step(block, carry):
        for sub in range(unroll):
            row = block * unroll + sub
            index = index_ref[pl.ds(row, 1), :]
            picked = fold_three(
                lax.dot_general(parts, one_hot_low(index), NN, preferred_element_type=F32)
            )
            hit = iota((high_count, 128), 0) == (index >> 7)
            out_ref[row] = jnp.sum(jnp.where(hit, picked, 0.0), axis=0, keepdims=True)
        return carry

    lax.fori_loop(0, index_ref.shape[0] // unroll, step, 0)


def scatter_rows(value_ref, index_ref, high_count, unroll):
    def step(block, total):
        for sub in range(unroll):
            row = block * unroll + sub
            index = index_ref[pl.ds(row, 1), :]
            hit = iota((high_count, 128), 0) == (index >> 7)
            parts = split_three(jnp.where(hit, value_ref[row], 0.0))
            total = total + lax.dot_general(
                parts, one_hot_low(index), NT, preferred_element_type=F32
            )
        return total

    start = jnp.zeros((3 * high_count, 128), F32)
    return fold_three(lax.fori_loop(0, index_ref.shape[0] // unroll, step, start))


def block_products(vectors, matrix_at, count, per_vector):
    rows = []
    for p in range(count):
        q = p // per_vector
        rows.append(
            lax.dot_general(
                vectors[q : q + 1],
                matrix_at(p),
                NT,
                precision=HIGHEST,
                preferred_element_type=F32,
            )
        )
    return jnp.concatenate(rows, axis=0)


def kernel(
    counts,
    source_hbm,
    mob_x_hbm,
    mob_y_hbm,
    mob_z_hbm,
    fraction_hbm,
    inverse_hbm,
    couplings_hbm,
    send_ref,
    recv_ref,
    near_row_ref,
    near_col_ref,
    out_x_hbm,
    out_r_hbm,
    res,
    mob_x,
    mob_y,
    mob_z,
    fraction,
    inverse,
    couplings,
    inv_diag,
    zed,
    direction,
    image,
    image_two,
    send_map,
    tile_table,
    back_table,
    low_mx,
    low_my,
    edge_my,
    edges,
    halo_x,
    halo_y,
    row_send,
    row_recv,
    link_send,
    link_recv,
    sum_send,
    sum_recv,
    load_sem,
    store_sem,
    side_send_sem,
    side_recv_sem,
    mob_send_sem,
    mob_recv_sem,
    row_send_sem,
    row_recv_sem,
    link_send_sem,
    link_recv_sem,
    sum_send_sem,
    sum_recv_sem,
):
    count_x, count_y = counts
    devices = count_x * count_y
    at_x, at_y = lax.axis_index("gx"), lax.axis_index("gy")
    me = at_x * count_y + at_y
    size_x, size_y, depth = res.shape
    tiles_z = depth // TZ
    group = 128 // (size_y * tiles_z)
    table_rows = size_x // group
    blocks = inverse.shape[0]
    push_count = near_row_ref.shape[1]
    unroll = 4

    loads = [
        pltpu.make_async_copy(src, dst, load_sem.at[n])
        for n, (src, dst) in enumerate(
            (
                (source_hbm, res),
                (fraction_hbm, fraction),
                (mob_y_hbm, mob_y),
                (mob_x_hbm, mob_x),
                (mob_z_hbm, mob_z),
                (inverse_hbm, inverse),
                (couplings_hbm, couplings),
            )
        )
    ]
    for load in loads:
        load.start()

    barrier = pltpu.get_barrier_semaphore()

    def peer(step):
        other = lax.rem(me + step, devices)
        return (other // count_y, lax.rem(other, count_y)), other

    def greet(step, carry):
        pl.semaphore_signal(barrier, inc=1, device_id=peer(step)[0], device_id_type=MESH)
        return carry

    low_mx[...] = jnp.zeros_like(low_mx)
    low_my[...] = jnp.zeros_like(low_my)
    halo_x[...] = jnp.zeros_like(halo_x)
    halo_y[...] = jnp.zeros_like(halo_y)
    lax.fori_loop(1, devices, greet, 0)

    def exchange(send, recv, send_sem, recv_sem, same=False):
        def one(step, carry):
            device, other = peer(step)
            pltpu.make_async_remote_copy(
                src_ref=send.at[0 if same else other],
                dst_ref=recv.at[me],
                send_sem=send_sem,
                recv_sem=recv_sem,
                device_id=device,
                device_id_type=MESH,
            ).start()
            return carry

        lax.fori_loop(1, devices, one, 0)
        recv[me] = send[0 if same else me]

    def arrived(recv, recv_sem):
        part = recv.at[pl.ds(0, devices - 1)]
        pltpu.make_async_copy(part, part, recv_sem).wait()

    tile = send_ref[...]
    low = tile & 127
    tile_k = low & (tiles_z - 1)
    tile_j = (low >> log2(tiles_z)) & (size_y - 1)
    tile_g = low >> log2(tiles_z * size_y)
    send_map[...] = (
        (tile - low) + tile_k * (group * size_y) + tile_g * size_y + tile_j
    )

    def stack_tiles(planes):
        return jnp.concatenate(
            [plane[:, k * TZ : (k + 1) * TZ] for k in range(tiles_z) for plane in planes],
            axis=0,
        )

    def total_tiles(alpha):
        def step(row, carry):
            planes = []
            for g in range(group):
                x = row * group + g
                plane = res[x]
                if alpha is not None:
                    plane = plane - alpha * image[x]
                    res[x] = plane
                planes.append(fraction[x] * plane)
            stacked = stack_tiles(planes)
            tile_table[pl.ds(row, 1), :] = jnp.sum(stacked.T, axis=0, keepdims=True)
            return carry

        lax.fori_loop(0, table_rows, step, 0)

    def coarse_send(phase, alpha):
        total_tiles(alpha)
        gather_rows(tile_table[...], send_map, row_send.at[2 * phase], unroll)

    def row_exchange(n):
        exchange(row_send.at[n], row_recv.at[n], row_send_sem.at[n], row_recv_sem.at[n])

    loads[0].wait()
    loads[1].wait()
    coarse_send(0, None)
    pl.semaphore_wait(barrier, devices - 1)
    row_exchange(0)

    near_row, near_col = near_row_ref[...], near_col_ref[...]
    target_row = near_row >> log2(blocks)
    target_col = near_col >> log2(blocks)
    earlier = iota((push_count, push_count), 0) < iota((push_count, push_count), 1)
    same = jnp.where((target_row == target_col) & earlier, 1, 0)
    rank = jnp.sum(same, axis=0, keepdims=True)
    slot = target_row * SLOT + rank
    chosen = iota((devices * SLOT, push_count), 0) == slot
    local = (near_row & (blocks - 1)).astype(F32)
    identity = jnp.sum(jnp.where(chosen, local, 0.0), axis=1, keepdims=True)
    link_send[0] = jnp.broadcast_to(identity, (devices * SLOT, 128)).reshape(
        devices, SLOT, 128
    )
    spread = jnp.where(chosen, 1.0, 0.0).astype(BF16)

    def link_exchange(n):
        exchange(link_send.at[n], link_recv.at[n], link_send_sem.at[n], link_recv_sem.at[n])

    link_exchange(0)

    def side_copy(src, dst, send_sem, recv_sem, shift_x, shift_y):
        return pltpu.make_async_remote_copy(
            src_ref=src,
            dst_ref=dst,
            send_sem=send_sem,
            recv_sem=recv_sem,
            device_id=(at_x + shift_x, at_y + shift_y),
            device_id_type=MESH,
        )

    loads[2].wait()
    loads[3].wait()

    def take_edge(x, carry):
        edge_my[x] = mob_y[x, size_y - 1 : size_y, :]
        return carry

    lax.fori_loop(0, size_x, take_edge, 0)
    copy_mx = side_copy(
        mob_x.at[size_x - 1], low_mx, mob_send_sem.at[0], mob_recv_sem.at[0], 1, 0
    )
    copy_my = side_copy(edge_my, low_my, mob_send_sem.at[1], mob_recv_sem.at[1], 0, 1)
    has_low_x, has_high_x = at_x > 0, at_x < count_x - 1
    has_low_y, has_high_y = at_y > 0, at_y < count_y - 1
    pl.when(has_high_x)(copy_mx.start)
    pl.when(has_high_y)(copy_my.start)

    lane = iota((size_y, depth), 1)
    row_of = iota((size_y, depth), 0)

    def below_z(plane):
        return jnp.where(lane == 0, 0.0, pltpu.roll(plane, 1, 1))

    def above_z(plane):
        return jnp.where(lane == depth - 1, 0.0, pltpu.roll(plane, depth - 1, 1))

    def below_y(plane, edge):
        return jnp.where(row_of == 0, edge, pltpu.roll(plane, 1, 0))

    def above_y(plane, edge):
        return jnp.where(row_of == size_y - 1, edge, pltpu.roll(plane, size_y - 1, 0))

    loads[4].wait()
    pl.when(has_low_x)(copy_mx.wait_recv)
    pl.when(has_low_y)(copy_my.wait_recv)

    def make_diagonal(x, lower):
        here = mob_x[x]
        mob_b, mob_c = mob_y[x], mob_z[x]
        value = (
            (here + lower)
            + (mob_b + below_y(mob_b, low_my[x]))
            + (mob_c + below_z(mob_c))
        )
        inv_diag[x] = 1.0 / value
        return here

    lax.fori_loop(0, size_x, make_diagonal, low_mx[...])

    def halo_copies(phase):
        out = []
        for side, (there, send, recv_here, shift_x, shift_y, came) in enumerate(
            (
                (has_low_x, 0, 1, -1, 0, has_high_x),
                (has_high_x, 1, 0, 1, 0, has_low_x),
                (has_low_y, 2, 1, 0, -1, has_high_y),
                (has_high_y, 3, 0, 0, 1, has_low_y),
            )
        ):
            field = zed if phase else direction
            if side < 2:
                src = field.at[0 if side == 0 else size_x - 1]
                dst = halo_x.at[phase, recv_here]
            else:
                src = edges.at[phase, side - 2]
                dst = halo_y.at[phase, recv_here]
            copy = side_copy(
                src,
                dst,
                side_send_sem.at[phase, side],
                side_recv_sem.at[phase, side],
                shift_x,
                shift_y,
            )
            out.append((there, came, copy))
        return out

    zero_plane = jnp.zeros((size_y, depth), F32)

    def precondition(phase):
        first, second = 2 * phase, 2 * phase + 1
        field = zed if phase else direction
        arrived(row_recv.at[first], row_recv_sem.at[first])
        totals = scatter_rows(row_recv.at[first], recv_ref, blocks, unroll)
        if phase == 0:
            loads[5].wait()
            loads[6].wait()
        sweep_one = block_products(totals, lambda p: inverse[p], blocks, 1)
        per_block = push_count // blocks
        pushed = block_products(sweep_one, lambda p: couplings[p], push_count, per_block)
        parts = split_three(pushed)
        out_values = jnp.zeros((devices * SLOT, 128), F32)
        for n in range(3):
            out_values = out_values + lax.dot_general(
                spread,
                parts[n * push_count : (n + 1) * push_count],
                NN,
                preferred_element_type=F32,
            )
        link_send[1 + phase] = out_values.reshape(devices, SLOT, 128)
        link_exchange(1 + phase)
        if phase == 0:
            arrived(link_recv.at[0], link_recv_sem.at[0])
        names = link_recv[0].reshape(devices * SLOT, 128).T[:blocks]
        gather_in = jnp.where(
            names == iota((blocks, devices * SLOT), 0).astype(F32), 1.0, 0.0
        ).astype(BF16)
        arrived(link_recv.at[1 + phase], link_recv_sem.at[1 + phase])
        values = split_three(link_recv[1 + phase].reshape(devices * SLOT, 128), axis=1)
        summed = lax.dot_general(gather_in, values, NN, preferred_element_type=F32)
        coupled = summed[:, :128] + summed[:, 128:256] + summed[:, 256:]
        sweep_two = block_products(totals - coupled, lambda p: inverse[p], blocks, 1)
        gather_rows(sweep_two, recv_ref, row_send.at[second], unroll)
        row_exchange(second)
        arrived(row_recv.at[second], row_recv_sem.at[second])
        back_table[...] = scatter_rows(row_recv.at[second], send_map, table_rows, unroll)

        def step(row, total):
            stacked = jnp.broadcast_to(back_table[pl.ds(row, 1), :], (128, 128)).T
            for g in range(group):
                x = row * group + g
                tiles = [
                    stacked[(k * group + g) * size_y : (k * group + g + 1) * size_y]
                    for k in range(tiles_z)
                ]
                here = res[x]
                value = fraction[x] * jnp.concatenate(tiles, axis=1) + here * inv_diag[x]
                field[x] = value
                edges[phase, 0, x] = value[0:1]
                edges[phase, 1, x] = value[size_y - 1 : size_y]
                total = total + here * value
            return total

        return jnp.sum(lax.fori_loop(0, table_rows, step, zero_plane))

    def apply_operator(phase, copies):
        field = zed if phase else direction
        result = image_two if phase else image
        for there, came, copy in copies:
            pl.when(there)(copy.start)
        for there, came, copy in copies:
            pl.when(came)(copy.wait_recv)

        def plane_step(x, below, here, above, lower):
            mob_a, mob_b, mob_c = mob_x[x], mob_y[x], mob_z[x]
            edge_low, edge_high = halo_y[phase, 0, x], halo_y[phase, 1, x]
            part_x = mob_a * (above - here) - lower * (here - below)
            part_y = mob_b * (above_y(here, edge_high) - here) - below_y(
                mob_b, low_my[x]
            ) * (here - below_y(here, edge_low))
            flux = mob_c * (above_z(here) - here)
            value = -(part_x + part_y + (flux - below_z(flux)))
            result[x] = value
            cross = value if phase == 0 else image[x]
            return here * value, here * cross, mob_a

        def step(x, carry):
            below, here, lower, total, cross = carry
            above = field[x + 1]
            one, two, lower = plane_step(x, below, here, above, lower)
            return here, above, lower, total + one, cross + two

        below, here, lower, total, cross = lax.fori_loop(
            0,
            size_x - 1,
            step,
            (halo_x[phase, 0], field[0], low_mx[...], zero_plane, zero_plane),
        )
        one, two, lower = plane_step(size_x - 1, below, here, halo_x[phase, 1], lower)
        return jnp.sum(total + one), jnp.sum(cross + two)

    def all_sums(phase, values):
        place = iota((1, 128), 1)
        row = jnp.zeros((1, 128), F32)
        for n, value in enumerate(values):
            row = jnp.where(place == n, value, row)
        sum_send[phase, 0] = row
        exchange(
            sum_send.at[phase],
            sum_recv.at[phase],
            sum_send_sem.at[phase],
            sum_recv_sem.at[phase],
            same=True,
        )
        arrived(sum_recv.at[phase], sum_recv_sem.at[phase])
        total = jnp.zeros((1, 128), F32)
        total = lax.fori_loop(
            0, devices, lambda n, total: total + sum_recv[phase, n], total
        )
        return [
            jnp.sum(jnp.where(place == n, total, 0.0), axis=1, keepdims=True)
            for n in range(len(values))
        ]

    copies_0, copies_1 = halo_copies(0), halo_copies(1)
    rz_part = precondition(0)
    energy_part, _ = apply_operator(0, copies_0)
    rz, energy = all_sums(0, (rz_part, energy_part))
    alpha = rz / energy

    coarse_send(1, alpha)
    row_exchange(2)
    next_part = precondition(1)
    own_part, cross_part = apply_operator(1, copies_1)
    rz_next, own, cross = all_sums(1, (next_part, own_part, cross_part))
    beta = rz_next / rz
    alpha_two = rz_next / (own + beta * (2.0 * cross + beta * energy))

    def finish(x, carry):
        first = direction[x]
        zed[x] = alpha * first + alpha_two * (zed[x] + beta * first)
        res[x] = res[x] - alpha_two * (image_two[x] + beta * image[x])
        return carry

    pl.when(has_high_x)(copy_mx.wait_send)
    pl.when(has_high_y)(copy_my.wait_send)
    for there, came, copy in copies_0 + copies_1:
        pl.when(there)(copy.wait_send)
    lax.fori_loop(0, size_x, finish, 0)
    stores = (
        pltpu.make_async_copy(zed, out_x_hbm, store_sem.at[0]),
        pltpu.make_async_copy(res, out_r_hbm, store_sem.at[1]),
    )
    for store in stores:
        store.start()
    for n in range(4):
        arrived(row_send.at[n], row_send_sem.at[n])
    for n in range(3):
        arrived(link_send.at[n], link_send_sem.at[n])
    for n in range(2):
        arrived(sum_recv.at[n], sum_send_sem.at[n])
    for store in stores:
        store.wait()


def body(
    source_term,
    mobility_x,
    mobility_y,
    mobility_z,
    bubble_fraction,
    tile_labels,
    send_tiles,
    recv_rows,
    block_inverse,
    couplings,
    neighbours,
):
    count_x, count_y = lax.axis_size("gx"), lax.axis_size("gy")
    devices = count_x * count_y
    size_x, size_y, depth = source_term.shape
    tiles = size_x * size_y * (depth // TZ)
    blocks, order = block_inverse.shape[:2]
    send, recv = send_tiles[0], recv_rows[0]
    pad = 128 - send.shape[1]
    assert order == 128 and pad >= 0
    if pad:
        send = jnp.pad(send, ((0, 0), (0, pad)), constant_values=tiles)
        recv = jnp.pad(recv, ((0, 0), (0, pad)), constant_values=blocks * order)
    push_count = neighbours.size
    table_rows = tiles // 128
    field = (size_x, size_y, depth)
    hbm = pl.BlockSpec(memory_space=pl.ANY)
    vmem = pl.BlockSpec(memory_space=pltpu.VMEM)
    dma = pltpu.SemaphoreType.DMA
    return pl.pallas_call(
        functools.partial(kernel, (count_x, count_y)),
        out_shape=(
            jax.ShapeDtypeStruct(field, F32),
            jax.ShapeDtypeStruct(field, F32),
        ),
        in_specs=[hbm] * 7 + [vmem] * 4,
        out_specs=(hbm, hbm),
        scratch_shapes=[
            pltpu.VMEM(field, F32),
            pltpu.VMEM(field, F32),
            pltpu.VMEM(field, F32),
            pltpu.VMEM(field, F32),
            pltpu.VMEM(field, F32),
            pltpu.VMEM((blocks, order, order), F32),
            pltpu.VMEM((push_count, order, order), F32),
            pltpu.VMEM(field, F32),
            pltpu.VMEM(field, F32),
            pltpu.VMEM(field, F32),
            pltpu.VMEM(field, F32),
            pltpu.VMEM(field, F32),
            pltpu.VMEM((devices, 128), jnp.int32),
            pltpu.VMEM((table_rows, 128), F32),
            pltpu.VMEM((table_rows, 128), F32),
            pltpu.VMEM((size_y, depth), F32),
            pltpu.VMEM((size_x, 1, depth), F32),
            pltpu.VMEM((size_x, 1, depth), F32),
            pltpu.VMEM((2, 2, size_x, 1, depth), F32),
            pltpu.VMEM((2, 2, size_y, depth), F32),
            pltpu.VMEM((2, 2, size_x, 1, depth), F32),
            pltpu.VMEM((4, devices, 1, 128), F32),
            pltpu.VMEM((4, devices, 1, 128), F32),
            pltpu.VMEM((3, devices, SLOT, 128), F32),
            pltpu.VMEM((3, devices, SLOT, 128), F32),
            pltpu.VMEM((2, 1, 1, 128), F32),
            pltpu.VMEM((2, devices, 1, 128), F32),
            dma((7,)),
            dma((2,)),
            dma((2, 4)),
            dma((2, 4)),
            dma((2,)),
            dma((2,)),
            dma((4,)),
            dma((4,)),
            dma((3,)),
            dma((3,)),
            dma((2,)),
            dma((2,)),
        ],
        compiler_params=pltpu.CompilerParams(
            collective_id=0, has_side_effects=True, vmem_limit_bytes=48 * 1024 * 1024
        ),
    )(
        source_term,
        mobility_x,
        mobility_y,
        mobility_z,
        bubble_fraction,
        block_inverse,
        couplings.reshape(push_count, order, order),
        send,
        recv,
        neighbours.reshape(1, push_count),
        neighbours.reshape(push_count, 1),
    )


def solution(mesh):
    return jax.shard_map(
        body,
        mesh=mesh,
        in_specs=(
            P("gx", "gy", None),
            P("gx", "gy", None),
            P("gx", "gy", None),
            P("gx", "gy", None),
            P("gx", "gy", None),
            P("gx", "gy", None),
            P(("gx", "gy"), None, None),
            P(("gx", "gy"), None, None),
            P(("gx", "gy"), None, None),
            P(("gx", "gy"), None, None, None),
            P(("gx", "gy"), None),
        ),
        out_specs=(P("gx", "gy", None), P("gx", "gy", None)),
        check_vma=False,
    )
```

time: 494 us -> 107 us (0.22)
  blocking collectives: 154 us -> 0 us
  other arithmetic: 127 us -> 0 us
  local copies, waits for them, and re-layouts: 125 us -> 7.97 us
  Pallas kernels: 0 us -> 97.9 us
  starting transfers between devices: 45 us -> 0 us
  waiting for transfers between devices: 23.4 us -> 0 us
  matrix products: 13.1 us -> 0 us
    psum x3 -> x0, blocking collectives: 124 us -> none  [inner_total(): return lax.psum(jnp.sum(left_field * right_field), ('gx', 'gy'))]
    pallas_call x0 -> x1, Pallas kernels: none -> 97.9 us  [body(): pl.pallas_call(functools.partial(kernel, (count_x, count_y)), out_shape=(...]
    gather x4 -> x0, local copies, waits for them, and re-layouts: 92.1 us -> none  [select_rows(): return jnp.take(values, positions, axis=0, mode='fill', fill_value=0.0)]
    scatter-add x6 -> x0, other arithmetic: 90.5 us -> none  [spread_rows(): return empty.at[positions].add(values, mode='drop')]
    all_to_all x3 -> x0, blocking collectives: 30.3 us -> none  [the longest x1 12.3 us: precondition(): lax.all_to_all(packed, ('gx', 'gy'), split_axis=0, concat_axis=0, tiled=T...]
    ppermute x10 -> x0, starting transfers between devices: 27.3 us -> none  [the longest x4 16.5 us: padded_2(): lax.ppermute(lax.slice_in_dim(block, block.shape[dim] - width, None, axis...]
    all_to_all x4 -> x0, waiting for transfers between devices: 20.1 us -> none  [the longest x1 7.4 us: precondition(): lax.all_to_all(out_values, ('gx', 'gy'), split_axis=0, concat_axis=0, til...]
    all_to_all x4 -> x0, starting transfers between devices: 17.7 us -> none  [the longest x1 7.33 us: precondition(): lax.all_to_all(out_ids, ('gx', 'gy'), split_axis=0, concat_axis=0, tiled=...]
  transfers between devices with their start and end apart: 14 -> 0, of which waited for: 7 -> 0; matrix products, arithmetic and copies ran while one was open for 24% -> 0% of each run, Pallas kernels for 0% -> 0%
where the time goes in v1:
time: 107 us; the launch traced here: 106 us
  Pallas kernels  97.9 us (91%)
  local copies, waits for them, and re-layouts  7.97 us (7%)
    pallas_call x1, Pallas kernels, body(): pl.pallas_call(functools.partial(kernel, (count_x, count_y)), out_shape=(...  97.9 us
    unnamed x13, local copies, waits for them, and re-layouts  7.81 us

profile of v1, /device:TPU:0, one launch (start us, length us, event | category | flops | bytes accessed | tf_op | source)
XLA Modules:
  0.0 106.5 jit_solution(14021930327279291485)
XLA Ops:
  0.6 0.8 copy.15
  1.4 0.1 reshape.14.near_row_ref
  1.5 0.1 reshape.16.near_col_ref
  1.5 0.0 copy-start
  1.5 1.2 %copy-done = f32[32,32,256]{2,1,0:T(8,128)S(1)} copy-done((f32[32,32,256]{2,1,0:T(8,128)S(1)}, f32[32,32,256]{2,1,0:T(8,128)}, u32[]{:S(2)}) %copy-start) | copy-done | bytes 1048600
  2.8 0.0 copy-start.1
  2.8 1.2 %copy-done.1 = f32[32,32,256]{2,1,0:T(8,128)S(1)} copy-done((f32[32,32,256]{2,1,0:T(8,128)S(1)}, f32[32,32,256]{2,1,0:T(8,128)}, u32[]{:S(2)}) %copy-start.1) | copy-done | bytes 1048600
  4.0 0.0 copy-start.2
  4.0 1.2 %copy-done.2 = f32[32,32,256]{2,1,0:T(8,128)S(1)} copy-done((f32[32,32,256]{2,1,0:T(8,128)S(1)}, f32[32,32,256]{2,1,0:T(8,128)}, u32[]{:S(2)}) %copy-start.2) | copy-done | bytes 1048600
  5.2 0.0 copy-start.3
  5.2 0.7 copy-done.3
  5.9 0.0 copy-start.4
  5.9 0.7 copy-done.4
  6.7 97.9 %shard_map.113 = (f32[32,32,256]{2,1,0:T(8,128)S(1)}, f32[32,32,256]{2,1,0:T(8,128)S(1)}) custom-call(f32[32,32,256]{2,1,0:T(8,128)S(1)} %copy-done, f32[32,32,256]{2,1,0:T(8,128)S(1)} %copy-done.1, f32[32,32,256]{2,1,0:T(8,128)S(1)} %copy-done.2, f32[32,32,256]{2,1,0:T(8,128)} %mob_z_hbm.1, f32[32,32,256]{2,1,0:T(8,128)} %fraction_hbm.1, ...), custom_call_target="tpu_custom_call" | custom-call | tf_op jit(solution)/shard_map/pallas_call | solution.py:557
  104.6 1.0 copy.20
  105.5 1.0 copy.21
Async XLA Ops:
  1.5 1.2 %copy-start = (f32[32,32,256]{2,1,0:T(8,128)S(1)}, f32[32,32,256]{2,1,0:T(8,128)}, u32[]{:S(2)}) copy-start(f32[32,32,256]{2,1,0:T(8,128)} %source_hbm.1) | copy-start | bytes 3145732
  2.8 1.2 %copy-start.1 = (f32[32,32,256]{2,1,0:T(8,128)S(1)}, f32[32,32,256]{2,1,0:T(8,128)}, u32[]{:S(2)}) copy-start(f32[32,32,256]{2,1,0:T(8,128)} %mob_x_hbm.1) | copy-start | bytes 3145732
  4.0 1.2 %copy-start.2 = (f32[32,32,256]{2,1,0:T(8,128)S(1)}, f32[32,32,256]{2,1,0:T(8,128)}, u32[]{:S(2)}) copy-start(f32[32,32,256]{2,1,0:T(8,128)} %mob_y_hbm.1) | copy-start | bytes 3145732
  5.2 0.7 copy-start.3
  5.9 0.7 copy-start.4

commit v2 on v1

--- a/solution.py
+++ b/solution.py
@@ -12,11 +12,10 @@
 SLOT = 8
 F32 = jnp.float32
 BF16 = jnp.bfloat16
-HIGHEST = lax.Precision.HIGHEST
 MESH = pl.DeviceIdType.MESH
 NT = (((1,), (1,)), ((), ()))
 NN = (((1,), (0,)), ((), ()))
-CELL_ARRAYS = 5
+GROUP = 8
 
 
 def log2(value):
@@ -28,71 +27,94 @@
     return lax.broadcasted_iota(jnp.int32, shape, axis)
 
 
-def split_three(value, axis=0):
-    first = value.astype(BF16)
-    rest = value - first.astype(F32)
-    second = rest.astype(BF16)
-    third = (rest - second.astype(F32)).astype(BF16)
-    return jnp.concatenate([first, second, third], axis=axis)
-
-
-def fold_three(value):
-    third = value.shape[0] // 3
-    return value[:third] + value[third : 2 * third] + value[2 * third :]
-
-
-def one_hot_low(index):
-    return jnp.where(iota((128, 128), 0) == (index & 127), 1.0, 0.0).astype(BF16)
-
-
-def gather_rows(table, index_ref, out_ref, unroll):
-    parts = split_three(table)
+def split_two(value):
+    first = value.astype(BF16).astype(F32)
+    return first, (value - first).astype(BF16).astype(F32)
+
+
+def stack_two(value, axis=0):
+    return jnp.concatenate(split_two(value), axis=axis).astype(BF16)
+
+
+def fold_two(value):
+    half = value.shape[0] // 2
+    return value[:half] + value[half:]
+
+
+def fold_tiles(value):
+    tiles = [
+        value[y : y + 8, z : z + 128]
+        for y in range(0, value.shape[0], 8)
+        for z in range(0, value.shape[1], 128)
+    ]
+    while len(tiles) > 1:
+        tiles = [a + b for a, b in zip(tiles[::2], tiles[1::2])]
+    return tiles[0]
+
+
+def write_one_hots(index_ref, hot_ref):
+    def step(block, carry):
+        for sub in range(GROUP):
+            index = index_ref[pl.ds(block * GROUP + sub, 1), :]
+            hot = jnp.where(iota((128, 128), 0) == (index & 127), 1.0, 0.0)
+            hot_ref[block, :, sub * 128 : (sub + 1) * 128] = hot.astype(BF16)
+        return carry
+
+    lax.fori_loop(0, hot_ref.shape[0], step, 0)
+
+
+def gather_rows(table, index_ref, hot_ref, out_ref):
+    parts = stack_two(table)
     high_count = table.shape[0]
 
     def step(block, carry):
-        for sub in range(unroll):
-            row = block * unroll + sub
-            index = index_ref[pl.ds(row, 1), :]
-            picked = fold_three(
-                lax.dot_general(parts, one_hot_low(index), NN, preferred_element_type=F32)
-            )
-            hit = iota((high_count, 128), 0) == (index >> 7)
-            out_ref[row] = jnp.sum(jnp.where(hit, picked, 0.0), axis=0, keepdims=True)
+        picked = fold_two(
+            lax.dot_general(parts, hot_ref[block], NN, preferred_element_type=F32)
+        )
+        for sub in range(GROUP):
+            row = block * GROUP + sub
+            hit = iota((high_count, 128), 0) == (index_ref[pl.ds(row, 1), :] >> 7)
+            mine = picked[:, sub * 128 : (sub + 1) * 128]
+            out_ref[row] = jnp.sum(jnp.where(hit, mine, 0.0), axis=0, keepdims=True)
         return carry
 
-    lax.fori_loop(0, index_ref.shape[0] // unroll, step, 0)
-
-
-def scatter_rows(value_ref, index_ref, high_count, unroll):
+    lax.fori_loop(0, hot_ref.shape[0], step, 0)
+
+
+def scatter_rows(value_ref, index_ref, hot_ref, high_count):
     def step(block, total):
-        for sub in range(unroll):
-            row = block * unroll + sub
-            index = index_ref[pl.ds(row, 1), :]
-            hit = iota((high_count, 128), 0) == (index >> 7)
-            parts = split_three(jnp.where(hit, value_ref[row], 0.0))
-            total = total + lax.dot_general(
-                parts, one_hot_low(index), NT, preferred_element_type=F32
-            )
-        return total
-
-    start = jnp.zeros((3 * high_count, 128), F32)
-    return fold_three(lax.fori_loop(0, index_ref.shape[0] // unroll, step, start))
-
-
-def block_products(vectors, matrix_at, count, per_vector):
-    rows = []
-    for p in range(count):
-        q = p // per_vector
-        rows.append(
-            lax.dot_general(
-                vectors[q : q + 1],
-                matrix_at(p),
-                NT,
-                precision=HIGHEST,
-                preferred_element_type=F32,
-            )
-        )
-    return jnp.concatenate(rows, axis=0)
+        pieces = []
+        for sub in range(GROUP):
+            row = block * GROUP + sub
+            hit = iota((high_count, 128), 0) == (index_ref[pl.ds(row, 1), :] >> 7)
+            pieces.append(stack_two(jnp.where(hit, value_ref[row], 0.0)))
+        return total + lax.dot_general(
+            jnp.concatenate(pieces, axis=1), hot_ref[block], NT, preferred_element_type=F32
+        )
+
+    start = jnp.zeros((2 * high_count, 128), F32)
+    return fold_two(lax.fori_loop(0, hot_ref.shape[0], step, start))
+
+
+def block_vectors(vectors):
+    first, second = split_two(vectors)
+    out = []
+    for q in range(vectors.shape[0]):
+        mine = iota(vectors.shape, 0) == q
+        top = jnp.where(mine, first, 0.0)
+        low = jnp.where(mine, second, 0.0)
+        upper = jnp.concatenate([top, top], axis=1)
+        lower = jnp.concatenate([low, jnp.zeros_like(low)], axis=1)
+        out.append(jnp.concatenate([upper, lower], axis=0).astype(BF16))
+    return out
+
+
+def block_products(vectors, split_ref):
+    total = None
+    for q, part in enumerate(block_vectors(vectors)):
+        term = lax.dot_general(part, split_ref[q], NT, preferred_element_type=F32)
+        total = term if total is None else total + term
+    return fold_two(total)
 
 
 def kernel(
@@ -122,6 +144,11 @@
     direction,
     image,
     image_two,
+    low_y,
+    inverse_split,
+    couplings_split,
+    send_hot,
+    recv_hot,
     send_map,
     tile_table,
     back_table,
@@ -160,7 +187,6 @@
     table_rows = size_x // group
     blocks = inverse.shape[0]
     push_count = near_row_ref.shape[1]
-    unroll = 4
 
     loads = [
         pltpu.make_async_copy(src, dst, load_sem.at[n])
@@ -248,11 +274,12 @@
 
     def coarse_send(phase, alpha):
         total_tiles(alpha)
-        gather_rows(tile_table[...], send_map, row_send.at[2 * phase], unroll)
+        gather_rows(tile_table[...], send_map, send_hot, row_send.at[2 * phase])
 
     def row_exchange(n):
         exchange(row_send.at[n], row_recv.at[n], row_send_sem.at[n], row_recv_sem.at[n])
 
+    write_one_hots(send_map, send_hot)
     loads[0].wait()
     loads[1].wait()
     coarse_send(0, None)
@@ -321,22 +348,33 @@
     def above_y(plane, edge):
         return jnp.where(row_of == size_y - 1, edge, pltpu.roll(plane, size_y - 1, 0))
 
-    loads[4].wait()
-    pl.when(has_low_x)(copy_mx.wait_recv)
-    pl.when(has_low_y)(copy_my.wait_recv)
+    write_one_hots(recv_ref, recv_hot)
+    loads[5].wait()
+
+    def split_inverse(q, carry):
+        inverse_split[q] = stack_two(inverse[q], axis=1)
+        return carry
+
+    lax.fori_loop(0, blocks, split_inverse, 0)
+    loads[6].wait()
+
+    def split_couplings(q, carry):
+        couplings_split[q] = stack_two(
+            jnp.concatenate([couplings[q, k] for k in range(couplings.shape[1])], axis=0),
+            axis=1,
+        )
+        return carry
+
+    lax.fori_loop(0, blocks, split_couplings, 0)
 
     def make_diagonal(x, lower):
         here = mob_x[x]
         mob_b, mob_c = mob_y[x], mob_z[x]
-        value = (
-            (here + lower)
-            + (mob_b + below_y(mob_b, low_my[x]))
-            + (mob_c + below_z(mob_c))
-        )
+        lower_b = below_y(mob_b, low_my[x])
+        low_y[x] = lower_b
+        value = (here + lower) + (mob_b + lower_b) + (mob_c + below_z(mob_c))
         inv_diag[x] = 1.0 / value
         return here
-
-    lax.fori_loop(0, size_x, make_diagonal, low_mx[...])
 
     def halo_copies(phase):
         out = []
@@ -366,45 +404,45 @@
             out.append((there, came, copy))
         return out
 
-    zero_plane = jnp.zeros((size_y, depth), F32)
+    zero_tile = jnp.zeros((8, 128), F32)
 
     def precondition(phase):
         first, second = 2 * phase, 2 * phase + 1
         field = zed if phase else direction
         arrived(row_recv.at[first], row_recv_sem.at[first])
-        totals = scatter_rows(row_recv.at[first], recv_ref, blocks, unroll)
-        if phase == 0:
-            loads[5].wait()
-            loads[6].wait()
-        sweep_one = block_products(totals, lambda p: inverse[p], blocks, 1)
-        per_block = push_count // blocks
-        pushed = block_products(sweep_one, lambda p: couplings[p], push_count, per_block)
-        parts = split_three(pushed)
-        out_values = jnp.zeros((devices * SLOT, 128), F32)
-        for n in range(3):
-            out_values = out_values + lax.dot_general(
-                spread,
-                parts[n * push_count : (n + 1) * push_count],
-                NN,
-                preferred_element_type=F32,
-            )
+        totals = scatter_rows(row_recv.at[first], recv_ref, recv_hot, blocks)
+        sweep_one = block_products(totals, inverse_split)
+        both = block_products(sweep_one, couplings_split)
+        pushed = jnp.concatenate(
+            [both[:, k * 128 : (k + 1) * 128] for k in range(couplings.shape[1])], axis=0
+        )
+        upper, lower = split_two(pushed)
+        out_values = lax.dot_general(
+            spread, upper.astype(BF16), NN, preferred_element_type=F32
+        ) + lax.dot_general(spread, lower.astype(BF16), NN, preferred_element_type=F32)
         link_send[1 + phase] = out_values.reshape(devices, SLOT, 128)
         link_exchange(1 + phase)
         if phase == 0:
+            loads[4].wait()
+            pl.when(has_low_x)(copy_mx.wait_recv)
+            pl.when(has_low_y)(copy_my.wait_recv)
+            lax.fori_loop(0, size_x, make_diagonal, low_mx[...])
             arrived(link_recv.at[0], link_recv_sem.at[0])
         names = link_recv[0].reshape(devices * SLOT, 128).T[:blocks]
         gather_in = jnp.where(
             names == iota((blocks, devices * SLOT), 0).astype(F32), 1.0, 0.0
         ).astype(BF16)
         arrived(link_recv.at[1 + phase], link_recv_sem.at[1 + phase])
-        values = split_three(link_recv[1 + phase].reshape(devices * SLOT, 128), axis=1)
+        values = stack_two(link_recv[1 + phase].reshape(devices * SLOT, 128), axis=1)
         summed = lax.dot_general(gather_in, values, NN, preferred_element_type=F32)
-        coupled = summed[:, :128] + summed[:, 128:256] + summed[:, 256:]
-        sweep_two = block_products(totals - coupled, lambda p: inverse[p], blocks, 1)
-        gather_rows(sweep_two, recv_ref, row_send.at[second], unroll)
+        coupled = summed[:, :128] + summed[:, 128:]
+        sweep_two = block_products(totals - coupled, inverse_split)
+        gather_rows(sweep_two, recv_ref, recv_hot, row_send.at[second])
         row_exchange(second)
         arrived(row_recv.at[second], row_recv_sem.at[second])
-        back_table[...] = scatter_rows(row_recv.at[second], send_map, table_rows, unroll)
+        back_table[...] = scatter_rows(
+            row_recv.at[second], send_map, send_hot, table_rows
+        )
 
         def step(row, total):
             stacked = jnp.broadcast_to(back_table[pl.ds(row, 1), :], (128, 128)).T
@@ -419,10 +457,10 @@
                 field[x] = value
                 edges[phase, 0, x] = value[0:1]
                 edges[phase, 1, x] = value[size_y - 1 : size_y]
-                total = total + here * value
+                total = total + fold_tiles(here * value)
             return total
 
-        return jnp.sum(lax.fori_loop(0, table_rows, step, zero_plane))
+        return jnp.sum(lax.fori_loop(0, table_rows, step, zero_tile))
 
     def apply_operator(phase, copies):
         field = zed if phase else direction
@@ -436,14 +474,14 @@
             mob_a, mob_b, mob_c = mob_x[x], mob_y[x], mob_z[x]
             edge_low, edge_high = halo_y[phase, 0, x], halo_y[phase, 1, x]
             part_x = mob_a * (above - here) - lower * (here - below)
-            part_y = mob_b * (above_y(here, edge_high) - here) - below_y(
-                mob_b, low_my[x]
-            ) * (here - below_y(here, edge_low))
+            part_y = mob_b * (above_y(here, edge_high) - here) - low_y[x] * (
+                here - below_y(here, edge_low)
+            )
             flux = mob_c * (above_z(here) - here)
             value = -(part_x + part_y + (flux - below_z(flux)))
             result[x] = value
-            cross = value if phase == 0 else image[x]
-            return here * value, here * cross, mob_a
+            one = fold_tiles(here * value)
+            return one, fold_tiles(here * image[x]) if phase else one, mob_a
 
         def step(x, carry):
             below, here, lower, total, cross = carry
@@ -455,7 +493,7 @@
             0,
             size_x - 1,
             step,
-            (halo_x[phase, 0], field[0], low_mx[...], zero_plane, zero_plane),
+            (halo_x[phase, 0], field[0], low_mx[...], zero_tile, zero_tile),
         )
         one, two, lower = plane_step(size_x - 1, below, here, halo_x[phase, 1], lower)
         return jnp.sum(total + one), jnp.sum(cross + two)
@@ -569,12 +607,17 @@
             pltpu.VMEM(field, F32),
             pltpu.VMEM(field, F32),
             pltpu.VMEM((blocks, order, order), F32),
-            pltpu.VMEM((push_count, order, order), F32),
-            pltpu.VMEM(field, F32),
-            pltpu.VMEM(field, F32),
-            pltpu.VMEM(field, F32),
-            pltpu.VMEM(field, F32),
-            pltpu.VMEM(field, F32),
+            pltpu.VMEM(couplings.shape, F32),
+            pltpu.VMEM(field, F32),
+            pltpu.VMEM(field, F32),
+            pltpu.VMEM(field, F32),
+            pltpu.VMEM(field, F32),
+            pltpu.VMEM(field, F32),
+            pltpu.VMEM(field, F32),
+            pltpu.VMEM((blocks, order, 2 * order), BF16),
+            pltpu.VMEM((blocks, order * couplings.shape[1], 2 * order), BF16),
+            pltpu.VMEM((devices // GROUP, 128, GROUP * 128), BF16),
+            pltpu.VMEM((devices // GROUP, 128, GROUP * 128), BF16),
             pltpu.VMEM((devices, 128), jnp.int32),
             pltpu.VMEM((table_rows, 128), F32),
             pltpu.VMEM((table_rows, 128), F32),
@@ -604,7 +647,7 @@
             dma((2,)),
         ],
         compiler_params=pltpu.CompilerParams(
-            collective_id=0, has_side_effects=True, vmem_limit_bytes=48 * 1024 * 1024
+            collective_id=0, has_side_effects=True, vmem_limit_bytes=63 * 1024 * 1024
         ),
     )(
         source_term,
@@ -613,11 +656,11 @@
         mobility_z,
         bubble_fraction,
         block_inverse,
-        couplings.reshape(push_count, order, order),
+        couplings,
         send,
         recv,
-        neighbours.reshape(1, push_count),
-        neighbours.reshape(push_count, 1),
+        neighbours.T.reshape(1, push_count),
+        neighbours.T.reshape(push_count, 1),
     )
 
 

time: 107 us -> 88.7 us (0.83)
  Pallas kernels: 97.9 us -> 81.7 us
  local copies, waits for them, and re-layouts: 7.97 us -> 6.01 us
    pallas_call x1, Pallas kernels: 97.9 us -> 81.7 us  [body(): pl.pallas_call(functools.partial(kernel, (count_x, count_y)), out_shape=(...]
    unnamed x13 -> x4, local copies, waits for them, and re-layouts: 7.81 us -> 3.37 us
    reshape x2, local copies, waits for them, and re-layouts: 0.16 us -> 2.64 us  [the longest x1 1.37 us: body(): neighbours.T.reshape(push_count, 1)]
where the time goes in v2:
time: 88.7 us; the launch traced here: 88.4 us
  Pallas kernels  81.7 us (92%)
  local copies, waits for them, and re-layouts  6.01 us (7%)
    pallas_call x1, Pallas kernels, body(): pl.pallas_call(functools.partial(kernel, (count_x, count_y)), out_shape=(...  81.7 us
    unnamed x4, local copies, waits for them, and re-layouts  3.37 us

profile of v2, /device:TPU:0, one launch (start us, length us, event | category | flops | bytes accessed | tf_op | source)
XLA Modules:
  0.0 88.4 jit_solution(2384894155772772500)
XLA Ops:
  0.6 1.3 %reshape.10.near_row_ref = s32[1,32]{1,0:T(1,128)} reshape(s32[2,16]{1,0:T(2,128)} %bitcast.5) | data formatting | bytes 256 | tf_op jit(solution)/shard_map/reshape | solution.py:662
  1.9 1.4 %reshape.12.near_col_ref = s32[32,1]{1,0:T(8,128)} reshape(s32[2,16]{1,0:T(2,128)} %bitcast.6) | data formatting | bytes 256 | tf_op jit(solution)/shard_map/reshape | solution.py:663
  3.3 81.7 %shard_map.113 = (f32[32,32,256]{2,1,0:T(8,128)}, f32[32,32,256]{2,1,0:T(8,128)}) custom-call(f32[32,32,256]{2,1,0:T(8,128)} %source_hbm.1, f32[32,32,256]{2,1,0:T(8,128)} %mob_x_hbm.1, f32[32,32,256]{2,1,0:T(8,128)} %mob_y_hbm.1, f32[32,32,256]{2,1,0:T(8,128)} %mob_z_hbm.1, f32[32,32,256]{2,1,0:T(8,128)} %fraction_hbm.1, f32[16,128,128]{2,1,0:T(8,128)} %inverse_hbm.1, ...), custom_call_target="tpu_custom_call" | custom-call | tf_op jit(solution)/shard_map/pallas_call | solution.py:595
  85.0 0.0 copy-start
  85.0 2.4 %copy.15 = f32[32,32,256]{2,1,0:T(8,128)} copy(f32[32,32,256]{2,1,0:T(8,128)} %get-tuple-element.4) | data formatting | bytes 2097152
  87.4 0.0 copy-done
  87.4 1.0 %copy.16 = f32[32,32,256]{2,1,0:T(8,128)} copy(f32[32,32,256]{2,1,0:T(8,128)S(1)} %copy-done) | data formatting | bytes 2097152
Async XLA Ops:
  85.0 2.4 %copy-start = (f32[32,32,256]{2,1,0:T(8,128)S(1)}, f32[32,32,256]{2,1,0:T(8,128)}, u32[]{:S(2)}) copy-start(f32[32,32,256]{2,1,0:T(8,128)} %get-tuple-element.5) | copy-start | bytes 3145732

commit v3 on v2

--- a/solution.py
+++ b/solution.py
@@ -9,7 +9,7 @@
 
 TZ = 128
 LINK = 4
-SLOT = 8
+SLOT = 4
 F32 = jnp.float32
 BF16 = jnp.bfloat16
 MESH = pl.DeviceIdType.MESH
@@ -128,10 +128,9 @@
     couplings_hbm,
     send_ref,
     recv_ref,
-    near_row_ref,
-    near_col_ref,
-    out_x_hbm,
-    out_r_hbm,
+    near_ref,
+    out_x,
+    out_r,
     res,
     mob_x,
     mob_y,
@@ -165,7 +164,6 @@
     sum_send,
     sum_recv,
     load_sem,
-    store_sem,
     side_send_sem,
     side_recv_sem,
     mob_send_sem,
@@ -186,7 +184,7 @@
     group = 128 // (size_y * tiles_z)
     table_rows = size_x // group
     blocks = inverse.shape[0]
-    push_count = near_row_ref.shape[1]
+    push_count = near_ref.size
 
     loads = [
         pltpu.make_async_copy(src, dst, load_sem.at[n])
@@ -256,24 +254,14 @@
             axis=0,
         )
 
-    def total_tiles(alpha):
+    def coarse_send(phase, field):
         def step(row, carry):
-            planes = []
-            for g in range(group):
-                x = row * group + g
-                plane = res[x]
-                if alpha is not None:
-                    plane = plane - alpha * image[x]
-                    res[x] = plane
-                planes.append(fraction[x] * plane)
+            planes = [fraction[x] * field[x] for x in [row * group + g for g in range(group)]]
             stacked = stack_tiles(planes)
             tile_table[pl.ds(row, 1), :] = jnp.sum(stacked.T, axis=0, keepdims=True)
             return carry
 
         lax.fori_loop(0, table_rows, step, 0)
-
-    def coarse_send(phase, alpha):
-        total_tiles(alpha)
         gather_rows(tile_table[...], send_map, send_hot, row_send.at[2 * phase])
 
     def row_exchange(n):
@@ -282,14 +270,17 @@
     write_one_hots(send_map, send_hot)
     loads[0].wait()
     loads[1].wait()
-    coarse_send(0, None)
+    coarse_send(0, res)
     pl.semaphore_wait(barrier, devices - 1)
     row_exchange(0)
 
-    near_row, near_col = near_row_ref[...], near_col_ref[...]
+    near_row = jnp.concatenate([near_ref[k : k + 1] for k in range(near_ref.shape[0])], axis=1)
     target_row = near_row >> log2(blocks)
-    target_col = near_col >> log2(blocks)
-    earlier = iota((push_count, push_count), 0) < iota((push_count, push_count), 1)
+    down, across = iota((push_count, push_count), 0), iota((push_count, push_count), 1)
+    target_col = jnp.sum(
+        jnp.where(down == across, target_row.astype(F32), 0.0), axis=1, keepdims=True
+    ).astype(jnp.int32)
+    earlier = down < across
     same = jnp.where((target_row == target_col) & earlier, 1, 0)
     rank = jnp.sum(same, axis=0, keepdims=True)
     slot = target_row * SLOT + rank
@@ -406,11 +397,14 @@
 
     zero_tile = jnp.zeros((8, 128), F32)
 
-    def precondition(phase):
-        first, second = 2 * phase, 2 * phase + 1
+    def coarse_totals(phase):
+        n = 2 * phase
+        arrived(row_recv.at[n], row_recv_sem.at[n])
+        return scatter_rows(row_recv.at[n], recv_ref, recv_hot, blocks)
+
+    def precondition(phase, totals):
+        second = 2 * phase + 1
         field = zed if phase else direction
-        arrived(row_recv.at[first], row_recv_sem.at[first])
-        totals = scatter_rows(row_recv.at[first], recv_ref, recv_hot, blocks)
         sweep_one = block_products(totals, inverse_split)
         both = block_products(sweep_one, couplings_split)
         pushed = jnp.concatenate(
@@ -467,15 +461,11 @@
         result = image_two if phase else image
         for there, came, copy in copies:
             pl.when(there)(copy.start)
-        for there, came, copy in copies:
-            pl.when(came)(copy.wait_recv)
-
         def plane_step(x, below, here, above, lower):
             mob_a, mob_b, mob_c = mob_x[x], mob_y[x], mob_z[x]
-            edge_low, edge_high = halo_y[phase, 0, x], halo_y[phase, 1, x]
             part_x = mob_a * (above - here) - lower * (here - below)
-            part_y = mob_b * (above_y(here, edge_high) - here) - low_y[x] * (
-                here - below_y(here, edge_low)
+            part_y = mob_b * (above_y(here, 0.0) - here) - low_y[x] * (
+                here - below_y(here, 0.0)
             )
             flux = mob_c * (above_z(here) - here)
             value = -(part_x + part_y + (flux - below_z(flux)))
@@ -489,17 +479,44 @@
             one, two, lower = plane_step(x, below, here, above, lower)
             return here, above, lower, total + one, cross + two
 
+        zero_plane = jnp.zeros((size_y, depth), F32)
         below, here, lower, total, cross = lax.fori_loop(
             0,
             size_x - 1,
             step,
-            (halo_x[phase, 0], field[0], low_mx[...], zero_tile, zero_tile),
-        )
-        one, two, lower = plane_step(size_x - 1, below, here, halo_x[phase, 1], lower)
-        return jnp.sum(total + one), jnp.sum(cross + two)
-
-    def all_sums(phase, values):
-        place = iota((1, 128), 1)
+            (zero_plane, field[0], low_mx[...], zero_tile, zero_tile),
+        )
+        one, two, lower = plane_step(size_x - 1, below, here, zero_plane, lower)
+        total, cross = total + one, cross + two
+
+        for there, came, copy in copies:
+            pl.when(came)(copy.wait_recv)
+        for x, weight, beside in (
+            (0, low_mx[...], halo_x[phase, 0]),
+            (size_x - 1, mob_x[size_x - 1], halo_x[phase, 1]),
+        ):
+            change = weight * beside
+            result[x] = result[x] - change
+            total = total - fold_tiles(field[x] * change)
+
+        def edge_step(block, total):
+            for sub in range(4):
+                x = block * 4 + sub
+                for y, weight, beside in (
+                    (0, low_y, halo_y[phase, 0, x]),
+                    (size_y - 1, mob_y, halo_y[phase, 1, x]),
+                ):
+                    change = weight[x, y : y + 1, :] * beside
+                    result[x, y : y + 1, :] = result[x, y : y + 1, :] - change
+                    total = total - field[x, y : y + 1, :] * change
+            return total
+
+        edge_total = lax.fori_loop(0, size_x // 4, edge_step, jnp.zeros((1, depth), F32))
+        return jnp.sum(total) + jnp.sum(edge_total), jnp.sum(cross)
+
+    place = iota((1, 128), 1)
+
+    def start_sums(phase, values):
         row = jnp.zeros((1, 128), F32)
         for n, value in enumerate(values):
             row = jnp.where(place == n, value, row)
@@ -511,55 +528,59 @@
             sum_recv_sem.at[phase],
             same=True,
         )
+
+    def end_sums(phase, count):
         arrived(sum_recv.at[phase], sum_recv_sem.at[phase])
-        total = jnp.zeros((1, 128), F32)
-        total = lax.fori_loop(
-            0, devices, lambda n, total: total + sum_recv[phase, n], total
-        )
+        totals = [sum_recv[phase, n] for n in range(4)]
+        for n in range(4, devices):
+            totals[n % 4] = totals[n % 4] + sum_recv[phase, n]
+        total = (totals[0] + totals[1]) + (totals[2] + totals[3])
         return [
             jnp.sum(jnp.where(place == n, total, 0.0), axis=1, keepdims=True)
-            for n in range(len(values))
+            for n in range(count)
         ]
 
     copies_0, copies_1 = halo_copies(0), halo_copies(1)
-    rz_part = precondition(0)
+    totals = coarse_totals(0)
+    rz_part = precondition(0, totals)
     energy_part, _ = apply_operator(0, copies_0)
-    rz, energy = all_sums(0, (rz_part, energy_part))
+    start_sums(0, (rz_part, energy_part))
+
+    coarse_send(1, image)
+    row_exchange(2)
+    rz, energy = end_sums(0, 2)
     alpha = rz / energy
 
-    coarse_send(1, alpha)
-    row_exchange(2)
-    next_part = precondition(1)
+    def update_residual(x, carry):
+        res[x] = res[x] - alpha * image[x]
+        return carry
+
+    lax.fori_loop(0, size_x, update_residual, 0)
+    totals = totals - alpha * coarse_totals(1)
+    next_part = precondition(1, totals)
     own_part, cross_part = apply_operator(1, copies_1)
-    rz_next, own, cross = all_sums(1, (next_part, own_part, cross_part))
+    start_sums(1, (next_part, own_part, cross_part))
+    rz_next, own, cross = end_sums(1, 3)
     beta = rz_next / rz
     alpha_two = rz_next / (own + beta * (2.0 * cross + beta * energy))
 
     def finish(x, carry):
         first = direction[x]
-        zed[x] = alpha * first + alpha_two * (zed[x] + beta * first)
-        res[x] = res[x] - alpha_two * (image_two[x] + beta * image[x])
+        out_x[x] = alpha * first + alpha_two * (zed[x] + beta * first)
+        out_r[x] = res[x] - alpha_two * (image_two[x] + beta * image[x])
         return carry
 
+    lax.fori_loop(0, size_x, finish, 0)
     pl.when(has_high_x)(copy_mx.wait_send)
     pl.when(has_high_y)(copy_my.wait_send)
     for there, came, copy in copies_0 + copies_1:
         pl.when(there)(copy.wait_send)
-    lax.fori_loop(0, size_x, finish, 0)
-    stores = (
-        pltpu.make_async_copy(zed, out_x_hbm, store_sem.at[0]),
-        pltpu.make_async_copy(res, out_r_hbm, store_sem.at[1]),
-    )
-    for store in stores:
-        store.start()
     for n in range(4):
         arrived(row_send.at[n], row_send_sem.at[n])
     for n in range(3):
         arrived(link_send.at[n], link_send_sem.at[n])
     for n in range(2):
         arrived(sum_recv.at[n], sum_send_sem.at[n])
-    for store in stores:
-        store.wait()
 
 
 def body(
@@ -586,10 +607,9 @@
     if pad:
         send = jnp.pad(send, ((0, 0), (0, pad)), constant_values=tiles)
         recv = jnp.pad(recv, ((0, 0), (0, pad)), constant_values=blocks * order)
-    push_count = neighbours.size
     table_rows = tiles // 128
     field = (size_x, size_y, depth)
-    hbm = pl.BlockSpec(memory_space=pl.ANY)
+    hbm = pl.BlockSpec(memory_space=pltpu.HBM)
     vmem = pl.BlockSpec(memory_space=pltpu.VMEM)
     dma = pltpu.SemaphoreType.DMA
     return pl.pallas_call(
@@ -598,8 +618,8 @@
             jax.ShapeDtypeStruct(field, F32),
             jax.ShapeDtypeStruct(field, F32),
         ),
-        in_specs=[hbm] * 7 + [vmem] * 4,
-        out_specs=(hbm, hbm),
+        in_specs=[hbm] * 7 + [vmem] * 3,
+        out_specs=(vmem, vmem),
         scratch_shapes=[
             pltpu.VMEM(field, F32),
             pltpu.VMEM(field, F32),
@@ -634,7 +654,6 @@
             pltpu.VMEM((2, 1, 1, 128), F32),
             pltpu.VMEM((2, devices, 1, 128), F32),
             dma((7,)),
-            dma((2,)),
             dma((2, 4)),
             dma((2, 4)),
             dma((2,)),
@@ -647,7 +666,7 @@
             dma((2,)),
         ],
         compiler_params=pltpu.CompilerParams(
-            collective_id=0, has_side_effects=True, vmem_limit_bytes=63 * 1024 * 1024
+            collective_id=0, has_side_effects=True, vmem_limit_bytes=63500000
         ),
     )(
         source_term,
@@ -659,8 +678,7 @@
         couplings,
         send,
         recv,
-        neighbours.T.reshape(1, push_count),
-        neighbours.T.reshape(push_count, 1),
+        neighbours.T,
     )
 
 

time: 88.7 us -> 75.3 us (0.85)
  Pallas kernels: 81.7 us -> 71.1 us
  local copies, waits for them, and re-layouts: 6.01 us -> 3.37 us
    pallas_call x1, Pallas kernels: 81.7 us -> 71.1 us  [body(): pl.pallas_call(functools.partial(kernel, (count_x, count_y)), out_shape=(...]
    reshape x2 -> x0, local copies, waits for them, and re-layouts: 2.64 us -> none  [the longest x1 1.37 us: body(): neighbours.T.reshape(push_count, 1)]
where the time goes in v3:
time: 75.3 us; the launch traced here: 75.1 us
  Pallas kernels  71.1 us (94%)
  local copies, waits for them, and re-layouts  3.37 us (4%)
    pallas_call x1, Pallas kernels, body(): pl.pallas_call(functools.partial(kernel, (count_x, count_y)), out_shape=(...  71.1 us
    unnamed x4, local copies, waits for them, and re-layouts  3.37 us

profile of v3, /device:TPU:0, one launch (start us, length us, event | category | flops | bytes accessed | tf_op | source)
XLA Modules:
  0.0 75.1 jit_solution(11087946450105874348)
XLA Ops:
  0.6 71.1 %shard_map.113 = (f32[32,32,256]{2,1,0:T(8,128)}, f32[32,32,256]{2,1,0:T(8,128)}) custom-call(f32[32,32,256]{2,1,0:T(8,128)} %source_hbm.1, f32[32,32,256]{2,1,0:T(8,128)} %mob_x_hbm.1, f32[32,32,256]{2,1,0:T(8,128)} %mob_y_hbm.1, f32[32,32,256]{2,1,0:T(8,128)} %mob_z_hbm.1, f32[32,32,256]{2,1,0:T(8,128)} %fraction_hbm.1, f32[16,128,128]{2,1,0:T(8,128)} %inverse_hbm.1, ...), custom_call_target="tpu_custom_call" | custom-call | tf_op jit(solution)/shard_map/pallas_call | solution.py:615
  71.7 0.0 copy-start
  71.7 2.4 %copy.14 = f32[32,32,256]{2,1,0:T(8,128)} copy(f32[32,32,256]{2,1,0:T(8,128)} %get-tuple-element.4) | data formatting | bytes 2097152
  74.1 0.0 copy-done
  74.1 1.0 %copy.15 = f32[32,32,256]{2,1,0:T(8,128)} copy(f32[32,32,256]{2,1,0:T(8,128)S(1)} %copy-done) | data formatting | bytes 2097152
Async XLA Ops:
  71.7 2.4 %copy-start = (f32[32,32,256]{2,1,0:T(8,128)S(1)}, f32[32,32,256]{2,1,0:T(8,128)}, u32[]{:S(2)}) copy-start(f32[32,32,256]{2,1,0:T(8,128)} %get-tuple-element.5) | copy-start | bytes 3145732

commit v4 on v3

--- a/solution.py
+++ b/solution.py
@@ -583,6 +583,11 @@
         arrived(sum_recv.at[n], sum_send_sem.at[n])
 
 
+def hand_on(x_ref, r_ref, out_x, out_r):
+    out_x[...] = x_ref[...]
+    out_r[...] = r_ref[...]
+
+
 def body(
     source_term,
     mobility_x,
@@ -612,7 +617,7 @@
     hbm = pl.BlockSpec(memory_space=pltpu.HBM)
     vmem = pl.BlockSpec(memory_space=pltpu.VMEM)
     dma = pltpu.SemaphoreType.DMA
-    return pl.pallas_call(
+    results = pl.pallas_call(
         functools.partial(kernel, (count_x, count_y)),
         out_shape=(
             jax.ShapeDtypeStruct(field, F32),
@@ -680,6 +685,14 @@
         recv,
         neighbours.T,
     )
+    part = pl.BlockSpec((size_x // 4, size_y, depth), lambda n: (n, 0, 0))
+    return pl.pallas_call(
+        hand_on,
+        grid=(4,),
+        out_shape=(jax.ShapeDtypeStruct(field, F32),) * 2,
+        in_specs=[part] * 2,
+        out_specs=(part, part),
+    )(*results)
 
 
 def solution(mesh):

time: 75.3 us -> 75.7 us (level)
  Pallas kernels: 71.1 us -> 74.8 us
  local copies, waits for them, and re-layouts: 3.37 us -> 0 us
    pallas_call x0 -> x1, Pallas kernels: none -> 3.75 us  [body(): pl.pallas_call(hand_on, grid=(4,), out_shape=(jax.ShapeDtypeStruct(field,...]
    unnamed x4 -> x0, local copies, waits for them, and re-layouts: 3.37 us -> none
where the time goes in v4:
time: 75.7 us; the launch traced here: 75.5 us
  Pallas kernels  74.8 us (99%)
    pallas_call x1, Pallas kernels, body(): pl.pallas_call(functools.partial(kernel, (count_x, count_y)), out_shape=(...  71.1 us
    pallas_call x1, Pallas kernels, body(): pl.pallas_call(hand_on, grid=(4,), out_shape=(jax.ShapeDtypeStruct(field,...  3.75 us

profile of v4, /device:TPU:0, one launch (start us, length us, event | category | flops | bytes accessed | tf_op | source)
XLA Modules:
  0.0 75.5 jit_solution(4631836184474859806)
XLA Ops:
  0.6 71.1 %shard_map.113 = (f32[32,32,256]{2,1,0:T(8,128)}, f32[32,32,256]{2,1,0:T(8,128)}) custom-call(f32[32,32,256]{2,1,0:T(8,128)} %source_hbm.1, f32[32,32,256]{2,1,0:T(8,128)} %mob_x_hbm.1, f32[32,32,256]{2,1,0:T(8,128)} %mob_y_hbm.1, f32[32,32,256]{2,1,0:T(8,128)} %mob_z_hbm.1, f32[32,32,256]{2,1,0:T(8,128)} %fraction_hbm.1, f32[16,128,128]{2,1,0:T(8,128)} %inverse_hbm.1, ...), custom_call_target="tpu_custom_call" | custom-call | tf_op jit(solution)/shard_map/pallas_call | solution.py:620
  71.7 3.8 %shard_map.114 = (f32[32,32,256]{2,1,0:T(8,128)}, f32[32,32,256]{2,1,0:T(8,128)}) custom-call(f32[32,32,256]{2,1,0:T(8,128)} %get-tuple-element.4.x_ref, f32[32,32,256]{2,1,0:T(8,128)} %get-tuple-element.5.r_ref), custom_call_target="tpu_custom_call" | custom-call | tf_op jit(solution)/shard_map/pallas_call | solution.py:689
